TPU v7x, 128 devices: a whole 4x4x4 slice. The times are simulated.
128 devices in a mesh: seq: 16 (over y, x), ctx: 8 (over z, core).
Axes of the slice: x: 4, y: 4, z: 4, core: 2. Of those that a mesh axis runs over, the one named last changes fastest.
Arguments:
- hidden_in: bfloat16 [16, 1024, 1024], P('seq', 'ctx'), may hold values from -6 to 6
- positions: int32 [16, 1024], P('seq', 'ctx'), may hold values from 0 to 1534, as said below
- starts: int32 [16, 2], P('seq'), may hold values from 0 to 768, as said below
- routes: int32 [16, 1024, 4], P('seq', 'ctx'), may hold values from 0 to 7, all different within a row; in each aligned block of 128 rows (0 to 127, 128 to 255, ..., all dimensions but the last counted through in order) at most 80 rows name the same one
- qkv_weight: bfloat16 [2048, 1024], P(('seq', 'ctx')), may hold values from -0.1875 to 0.1875
- out_weight: bfloat16 [1024, 1024], P(('seq', 'ctx')), may hold values from -1.5 to 1.5
- expert_in: bfloat16 [1024, 8, 1024], P(('seq', 'ctx')), may hold values from -0.1875 to 0.1875
- expert_out: bfloat16 [1024, 8, 512], P(('seq', 'ctx')), may hold values from -1.5 to 1.5
- router: bfloat16 [1024, 8], replicated, may hold values from -0.09375 to 0.09375
- attn_gain: bfloat16 [1024], replicated, may hold values from 0.25 to 1.75
- query_gain: bfloat16 [1024], replicated, may hold values from 0.25 to 1.75
- key_gain: bfloat16 [512], replicated, may hold values from 0.25 to 1.75
- mlp_gain: bfloat16 [1024], replicated, may hold values from 0.25 to 1.75
- out_grad: bfloat16 [16, 1024, 1024], P('seq', 'ctx'), may hold values from -6 to 6
Outputs:
- result: bfloat16 [16, 1024, 1024], P('seq', 'ctx')
- grad_input: float32 [16, 1024, 1024], P('seq', 'ctx')
- grad_qkv: float32 [2048, 1024], P(('seq', 'ctx'))
- grad_out: float32 [1024, 1024], P(('seq', 'ctx'))
- grad_expert_in: float32 [1024, 8, 1024], P(('seq', 'ctx'))
- grad_expert_out: float32 [1024, 8, 512], P(('seq', 'ctx'))
- grad_router: float32 [1024, 8], replicated
- grad_attn_gain: float32 [1024], replicated
- grad_query_gain: float32 [1024], replicated
- grad_key_gain: float32 [512], replicated
- grad_mlp_gain: float32 [1024], replicated
Inputs may be any that keep to these rules, and one draw needn't show every extreme that they name: `routes`: each row names 4 different experts; among the 128 tokens of one sequence on one device (aligned blocks), no expert is named by more than 80 of them. Piece k of a sequence starts at a token index from k * 512 to (k + 1) * 512 - 256; pieces never intersect. Within a sequence positions start at 0 and rise by 1 or 2 from token to token; the last token of every sequence has position 1534.
All inputs are finite; a program needn't handle non-finite values.
Results may differ from a plain program's by a relative error of at most 0.018.
Values may be sent and summed in bfloat16 or wider, within the bound.
A program may use at most 256 MiB of HBM per device.

v0:
```python
import jax
import jax.numpy as jnp
import numpy as np
from jax import lax
from jax.sharding import PartitionSpec as P

QUERY_HEADS = 16
KEY_VALUE_HEADS = 8
PIECE = 256
EPSILON = 1e-06
ROPE_BASE = 10000.0
MASKED = -1e30
F32 = jnp.float32
BF16 = jnp.bfloat16


def rms_scale(field):
    return lax.rsqrt(jnp.mean(field * field, axis=-1, keepdims=True) + EPSILON)


def rms_back(upstream, normed, scales):
    return scales * (upstream - normed * jnp.mean(upstream * normed, axis=-1, keepdims=True))


def rotary(field, cosine, sine):
    half = field.shape[-1] // 2
    a, b = (field[..., :half], field[..., half:])
    return jnp.concatenate([a * cosine - b * sine, b * cosine + a * sine], axis=-1)


def owner_of(s, c):
    if s < 8:
        return 8 * c + s
    if s < 12:
        return 64 + 4 * c + (s - 8)
    return 96 + 4 * c + (s - 12)


def dot(a, b, ca, cb):
    return lax.dot_general(a, b, (((ca,), (cb,)), ((), ())), preferred_element_type=F32)


def local(
    hidden_in,
    positions,
    starts,
    routes,
    qkv_weight,
    out_weight,
    expert_in,
    expert_out,
    router,
    attn_gain,
    query_gain,
    key_gain,
    mlp_gain,
    out_grad,
):
    rows = hidden_in.shape[1]
    width = hidden_in.shape[2]
    me = lax.axis_index("ctx")
    ns, nc = (lax.axis_size("seq"), lax.axis_size("ctx"))
    perm_in = [(owner_of(s, c), s * nc + c) for s in range(ns) for c in range(nc)]
    perm_out = [(b, a) for a, b in perm_in]
    ag = lambda v, ax: lax.all_gather(v, ax, axis=0, tiled=True)
    a2a = lambda v, sp, cc: lax.all_to_all(v, "ctx", sp, cc, tiled=True)
    w_qkv = ag(lax.ppermute(qkv_weight, ("seq", "ctx"), perm_in), "seq")
    w_out = ag(a2a(out_weight, 1, 0), "seq")
    w_in = ag(a2a(expert_in, 1, 0)[:, 0], "seq")
    w_down = ag(a2a(expert_out, 1, 0)[:, 0], "seq")
    x_own = hidden_in[0].astype(F32)
    x = ag(hidden_in[0], "ctx").astype(F32)
    dy = ag(out_grad[0], "ctx").astype(F32)
    pos = ag(positions[0], "ctx")
    routes_all = ag(routes[0], "ctx")
    s1 = rms_scale(x)
    attn_gain_f = attn_gain.astype(F32)
    x_low = (x * s1 * attn_gain_f).astype(BF16)
    qkv = dot(x_low, w_qkv, 1, 1)
    q, k, v = (qkv[:, :128], qkv[:, 128:192], qkv[:, 192:])
    sums = lax.psum(jnp.stack([jnp.sum(q * q, 1), jnp.sum(k * k, 1)]), "ctx")
    sq = lax.rsqrt(sums[0] / 1024 + EPSILON)[:, None]
    sk = lax.rsqrt(sums[1] / 512 + EPSILON)[:, None]
    nq, nk = (q * sq, k * sk)
    gq = lax.dynamic_slice(query_gain, (128 * me,), (128,)).astype(F32)
    gk = lax.dynamic_slice(key_gain, (64 * me,), (64,)).astype(F32)
    freq = ROPE_BASE ** (-jnp.arange(32, dtype=F32) * 2.0 / 64)
    ang = pos.astype(F32)[:, None] * freq
    cosv, sinv = (jnp.cos(ang), jnp.sin(ang))
    q_rot = rotary((nq * gq).reshape(-1, 2, 64), cosv[:, None], sinv[:, None]).astype(BF16)
    k_rot = rotary(nk * gk, cosv, sinv).astype(BF16)
    v_low = v.astype(BF16)
    places = jnp.arange(pos.shape[0], dtype=jnp.int32)
    inside = (places[:, None] >= starts) & (places[:, None] < starts + PIECE)
    label = jnp.sum(inside.astype(jnp.int32) * jnp.array([1, 2], jnp.int32), axis=1)
    allowed = (places[None, :] <= places[:, None]) | (label[:, None] == label[None, :]) & (
        label[:, None] > 0
    )
    scores = jnp.einsum("tgd,sd->gts", q_rot, k_rot, preferred_element_type=F32) * 0.125
    scores = jnp.where(allowed[None], scores, MASKED)
    p = jax.nn.softmax(scores, axis=-1)
    p_low = p.astype(BF16)
    attn = jnp.einsum("gts,sd->tgd", p_low, v_low, preferred_element_type=F32)
    attn_low = attn.reshape(-1, 128).astype(BF16)
    rs = lambda t: lax.psum_scatter(t, "ctx", scatter_dimension=0, tiled=True)
    mid = x_own + rs(dot(attn_low, w_out, 1, 1))
    s2 = rms_scale(mid)
    n2 = mid * s2
    gm = mlp_gain.astype(F32)
    h_own = (n2 * gm).astype(BF16)
    gates_own = jax.nn.softmax(jnp.dot(h_own, router, preferred_element_type=F32), axis=-1)
    h = ag(h_own, "ctx")
    gates = ag(gates_own, "ctx")
    routed = jnp.any(routes_all == me, axis=1)
    gate_c = jnp.where(routed, lax.dynamic_slice(gates, (0, me), (gates.shape[0], 1))[:, 0], 0.0)[
        :, None
    ]
    gu = dot(h, w_in, 1, 0)
    g, u = (gu[:, :512], gu[:, 512:])
    sig = jax.nn.sigmoid(g)
    sw = g * sig
    act = (sw * u).astype(BF16)
    res = dot(act, w_down, 1, 1)
    result = (mid + rs(gate_c * res)).astype(BF16)[None]
    d_res = (gate_c * dy).astype(BF16)
    d_gate_c = jnp.where(routed, jnp.sum(dy * res, axis=1), 0.0)
    d_act = dot(d_res, w_down, 1, 0)
    d_gu = jnp.concatenate([d_act * u * sig * (1.0 + g * (1.0 - sig)), d_act * sw], axis=1).astype(
        BF16
    )
    d_h = rs(dot(d_gu, w_in, 1, 1))
    g_in = dot(h, d_gu, 0, 0)
    g_down = dot(d_res, act, 0, 0)
    d_gates = a2a(d_gate_c[:, None], 0, 1)
    d_logits = (gates_own * (d_gates - jnp.sum(gates_own * d_gates, axis=1, keepdims=True))).astype(
        BF16
    )
    d_h = d_h + dot(d_logits, router, 1, 1)
    router_loc = dot(h_own, d_logits, 0, 0)
    mlp_loc = jnp.sum(d_h * n2, axis=0)
    d_mid = out_grad[0].astype(F32) + rms_back(d_h * gm, n2, s2)
    d_branch_own = d_mid.astype(BF16)
    d_branch = ag(d_branch_own, "ctx")
    d_attn = dot(d_branch, w_out, 1, 0).astype(BF16)
    g_out = dot(d_branch, attn_low, 0, 0)
    dp = jnp.einsum("tgd,sd->gts", d_attn.reshape(-1, 2, 64), v_low, preferred_element_type=F32)
    ds = (p * (dp - jnp.sum(p * dp, axis=-1, keepdims=True))).astype(BF16)
    dq = jnp.einsum("gts,sd->tgd", ds, k_rot, preferred_element_type=F32) * 0.125
    dk = jnp.einsum("gts,tgd->sd", ds, q_rot, preferred_element_type=F32) * 0.125
    dv = jnp.einsum("gts,tgd->sd", p_low, d_attn.reshape(-1, 2, 64), preferred_element_type=F32)
    dnq = rotary(dq, cosv[:, None], -sinv[:, None]).reshape(-1, 128)
    dnk = rotary(dk, cosv, -sinv)
    gq_loc = jnp.sum(dnq * nq, axis=0)
    gk_loc = jnp.sum(dnk * nk, axis=0)
    means = lax.psum(jnp.stack([jnp.sum(dnq * gq * nq, 1), jnp.sum(dnk * gk * nk, 1)]), "ctx")
    d_q = sq * (dnq * gq - nq * means[0][:, None] / 1024)
    d_k = sk * (dnk * gk - nk * means[1][:, None] / 512)
    d_qkv = jnp.concatenate([d_q, d_k, dv], axis=1).astype(BF16)
    d_x_low = rs(dot(d_qkv, w_qkv, 1, 0))
    g_qkv = dot(d_qkv, x_low, 0, 0)
    s1_own = rms_scale(x_own)
    n1_own = x_own * s1_own
    attn_loc = jnp.sum(d_x_low * n1_own, axis=0)
    grad_input = (d_mid + rms_back(d_x_low * attn_gain_f, n1_own, s1_own))[None]
    rss = lambda t: lax.psum_scatter(t, "seq", scatter_dimension=0, tiled=True)
    grad_qkv = lax.ppermute(rss(g_qkv), ("seq", "ctx"), perm_out)
    grad_out = a2a(rss(g_out), 0, 1)
    grad_in = a2a(rss(g_in)[:, None], 0, 1)
    grad_down = a2a(rss(g_down)[:, None], 0, 1)
    gq_all = lax.dynamic_update_slice(jnp.zeros((1024,), F32), gq_loc, (128 * me,))
    gk_all = lax.dynamic_update_slice(jnp.zeros((512,), F32), gk_loc, (64 * me,))
    ga, gqo, gko, gmo, gr = lax.psum(
        (attn_loc, gq_all, gk_all, mlp_loc, router_loc), ("seq", "ctx")
    )
    return (result, grad_input, grad_qkv, grad_out, grad_in, grad_down, gr, ga, gqo, gko, gmo)


def solution(mesh):
    t = ("seq", "ctx")
    in_specs = (
        P("seq", "ctx", None),
        P("seq", "ctx"),
        P("seq", None),
        P("seq", "ctx", None),
        P(t, None),
        P(t, None),
        P(t, None, None),
        P(t, None, None),
        P(),
        P(),
        P(),
        P(),
        P(),
        P("seq", "ctx", None),
    )
    out_specs = (
        P("seq", "ctx", None),
        P("seq", "ctx", None),
        P(t, None),
        P(t, None),
        P(t, None, None),
        P(t, None, None),
        P(),
        P(),
        P(),
        P(),
        P(),
    )
    return jax.shard_map(local, mesh=mesh, in_specs=in_specs, out_specs=out_specs, check_vma=False)
```

profile of v0, /device:TPU:1, one launch (start us, length us, event | category | flops | bytes accessed | tf_op | source)
XLA Modules:
  0.0 795.4 jit_solution(15250596640842094345)
XLA Ops:
  8.8 6.8 all-to-all-start
  23.7 13.3 %all-gather.1 = s32[1,1024]{1,0:T(1,128)S(1)} all-gather(s32[1,128]{1,0:T(1,128)} %param.16), channel_id=3, replica_groups=mesh['seq'=16,'ctx'=8] {'ctx'}, dimensions={1}, use_global_device_ids=true | all-gather | bytes 4608 | tf_op jit(solution)/shard_map/all_gather | solution.py:65
  37.6 17.3 %all_gather.36 = bf16[1024,128]{1,0:T(8,128)(2,1)S(1)} all-gather(bf16[64,128]{1,0:T(8,128)(2,1)S(1)} %bitcast.193), channel_id=1, replica_groups=mesh['seq'=16,'ctx'=8] {'seq'}, dimensions={0}, use_global_device_ids=true | all-gather | bytes 278528 | tf_op jit(solution)/shard_map/all_gather | solution.py:65
  54.9 17.4 %all_gather.34 = bf16[256,1024]{1,0:T(8,128)(2,1)S(1)} all-gather(bf16[16,1024]{1,0:T(8,128)(2,1)S(1)} %collective-permute-done), channel_id=1, replica_groups=mesh['seq'=16,'ctx'=8] {'seq'}, dimensions={0}, use_global_device_ids=true | all-gather | bytes 557056 | tf_op jit(solution)/shard_map/all_gather | solution.py:65
  77.2 22.6 %psum.49 = f32[2,1024]{1,0:T(2,128)S(1)} all-reduce(f32[2,1024]{1,0:T(2,128)S(1)} %pad_maximum_fusion.16), channel_id=1, replica_groups=mesh['seq'=16,'ctx'=8] {'ctx'}, use_global_device_ids=true, to_apply=%region_4.0 | all-reduce | flops 2048 | bytes 16384 | tf_op jit(solution)/shard_map/psum | solution.py:81
  102.1 5.4 fusion.97
  114.8 9.5 %all_to_all.120 = bf16[8,8,1024]{2,0,1:T(8,128)(2,1)} all-to-all(bf16[8,8,1024]{2,0,1:T(8,128)(2,1)S(1)} %copy.58), channel_id=1, replica_groups=mesh['seq'=16,'ctx'=8] {'ctx'}, dimensions={1} | all-to-all | bytes 262144 | tf_op jit(solution)/shard_map/all_to_all | solution.py:66
  124.5 22.8 %reduce-scatter.9.cloned.1.call-done = f32[128,1024]{1,0:T(8,128)} async-done(((f32[1024,1024]{1,0:T(8,128)}), f32[128,1024]{1,0:T(8,128)}) %reduce-scatter.9.cloned.1.call-update) | async-done | bytes 524304 | tf_op jit(solution)/shard_map/reduce_scatter | solution.py:105
  150.1 11.8 %all_to_all.121 = bf16[8,8,512]{2,0,1:T(8,128)(2,1)} all-to-all(bf16[8,8,512]{2,0,1:T(8,128)(2,1)S(1)} %copy.59), channel_id=1, replica_groups=mesh['seq'=16,'ctx'=8] {'ctx'}, dimensions={1} | all-to-all | bytes 131072 | tf_op jit(solution)/shard_map/all_to_all | solution.py:66
  162.7 12.3 %all-gather.2 = s32[1,1024,4]{1,2,0:T(4,128)S(1)} all-gather(s32[1,128,4]{1,2,0:T(4,128)S(1)} %copy-done.52), channel_id=4, replica_groups=mesh['seq'=16,'ctx'=8] {'ctx'}, dimensions={1}, use_global_device_ids=true | all-gather | bytes 18432 | tf_op jit(solution)/shard_map/all_gather | solution.py:65
  176.1 17.3 %all-gather.11.cloned.1.call-done = bf16[1024,1024]{1,0:T(8,128)(2,1)} async-done(((bf16[128,1024]{1,0:T(8,128)(2,1)}), bf16[1024,1024]{1,0:T(8,128)(2,1)}) %all-gather.11.cloned.1.call-update) | async-done | bytes 2097168 | tf_op jit(solution)/shard_map/all_gather | solution.py:65
  193.5 6.5 fusion.100
  202.8 33.4 %all-gather.15.cloned.1.call-done = bf16[1024,512]{1,0:T(8,128)(2,1)} async-done(((bf16[64,512]{1,0:T(8,128)(2,1)}), bf16[1024,512]{1,0:T(8,128)(2,1)}) %all-gather.15.cloned.1.call-update) | async-done | bytes 1048592 | tf_op jit(solution)/shard_map/all_gather | solution.py:65
  236.2 28.7 %all-gather.21.cloned.1.call-done = bf16[1,1024,1024]{2,1,0:T(8,128)(2,1)} async-done(((bf16[1,128,1024]{2,1,0:T(8,128)(2,1)}), bf16[1,1024,1024]{2,1,0:T(8,128)(2,1)}) %all-gather.21.cloned.1.call-update) | async-done | bytes 2097168 | tf_op jit(solution)/shard_map/all_gather | solution.py:65
  264.8 5.2 fusion.9
  278.7 13.3 %all_gather.38 = f32[1024,8]{0,1:T(8,128)S(1)} all-gather(f32[128,8]{0,1:T(8,128)S(1)} %get-tuple-element.25), channel_id=1, replica_groups=mesh['seq'=16,'ctx'=8] {'ctx'}, dimensions={0}, use_global_device_ids=true | all-gather | bytes 36864 | tf_op jit(solution)/shard_map/all_gather | solution.py:65
  292.0 5.4 multiply_convert_fusion.1
  303.8 33.8 %reduce-scatter.13.cloned.1.call-done = f32[128,1024]{1,0:T(8,128)} async-done(((f32[1024,1024]{1,0:T(8,128)}), f32[128,1024]{1,0:T(8,128)}) %reduce-scatter.13.cloned.1.call-update) | async-done | bytes 524304 | tf_op jit(solution)/shard_map/reduce_scatter | solution.py:105
  346.3 6.5 fusion.19
  352.9 16.5 %all-gather.17.cloned.1.call-done = bf16[1024,1024]{1,0:T(8,128)(2,1)} async-done(((bf16[128,1024]{1,0:T(8,128)(2,1)}), bf16[1024,1024]{1,0:T(8,128)(2,1)}) %all-gather.17.cloned.1.call-update) | async-done | bytes 2097168 | tf_op jit(solution)/shard_map/all_gather | solution.py:65
  384.6 12.2 %psum.50 = f32[2,1024]{1,0:T(2,128)S(1)} all-reduce(f32[2,1024]{1,0:T(2,128)S(1)} %pad_maximum_fusion.17), channel_id=1, replica_groups=mesh['seq'=16,'ctx'=8] {'ctx'}, use_global_device_ids=true, to_apply=%region_21.22 | all-reduce | flops 2048 | bytes 16384 | tf_op jit(solution)/shard_map/psum | solution.py:155
  398.4 5.0 fusion.29
  417.6 27.3 %reduce-scatter.23.cloned.1.call-done = f32[64,512]{1,0:T(8,128)} async-done(((f32[1024,512]{1,0:T(8,128)}), f32[64,512]{1,0:T(8,128)}) %reduce-scatter.23.cloned.1.call-update) | async-done | bytes 131088 | tf_op jit(solution)/shard_map/reduce_scatter | solution.py:165
  446.6 6.8 all-to-all-start.6
  453.3 72.0 %reduce-scatter.21.cloned.1.call-done = f32[64,1024]{1,0:T(8,128)} async-done(((f32[1024,1024]{1,0:T(8,128)}), f32[64,1024]{1,0:T(8,128)}) %reduce-scatter.21.cloned.1.call-update) | async-done | bytes 262160 | tf_op jit(solution)/shard_map/reduce_scatter | solution.py:165
  527.3 6.8 all-to-all-start.5
  534.1 66.5 %reduce-scatter.17.cloned.1.call-done = f32[16,1024]{1,0:T(8,128)} async-done(((f32[256,1024]{1,0:T(8,128)}), f32[16,1024]{1,0:T(8,128)}) %reduce-scatter.17.cloned.1.call-update) | async-done | bytes 65552 | tf_op jit(solution)/shard_map/reduce_scatter | solution.py:165
  600.6 5.0 collective-permute-start.1
  605.6 69.8 %reduce-scatter.19.cloned.1.call-done = f32[64,128]{1,0:T(8,128)} async-done(((f32[1024,128]{1,0:T(8,128)}), f32[64,128]{1,0:T(8,128)}) %reduce-scatter.19.cloned.1.call-update) | async-done | bytes 32784 | tf_op jit(solution)/shard_map/reduce_scatter | solution.py:165
  675.4 7.0 all-to-all-start.4
  687.1 26.9 %reduce-scatter.15.cloned.1.call-done = f32[128,1024]{1,0:T(8,128)} async-done(((f32[1024,1024]{1,0:T(8,128)}), f32[128,1024]{1,0:T(8,128)}) %reduce-scatter.15.cloned.1.call-update) | async-done | bytes 524304 | tf_op jit(solution)/shard_map/reduce_scatter | solution.py:105
  715.4 68.8 %all-reduce = (f32[1024,8]{0,1:T(8,128)}, f32[1024]{0:T(1024)}, f32[1024]{0:T(1024)}, f32[512]{0:T(512)}, f32[1024]{0:T(1024)}) all-reduce(f32[1024,8]{0,1:T(8,128)S(1)} %fusion.102, f32[1024]{0:T(1024)S(1)} %get-tuple-element.17, f32[1024]{0:T(1024)S(1)} %dynamic_update_slice.6, ...), channel_id=1, replica_groups=mesh['seq'=16,'ctx'=8] {'seq','ctx'}, use_global_device_ids=true, to_apply=%region_28.29 | all-reduce | flops 11776 | bytes 94208 | tf_op jit(solution)/shard_map/psum | solution.py:172
  (239 shorter events, 98.6 us)
Async XLA Ops:
  8.0 64.3 %all-gather.19.cloned.1.call-start = ((), (), s32[]{:S(2)}) async-start(), calls=%async_computation.27 | async-start | bytes 2359296 | tf_op jit(solution)/shard_map/all_gather | solution.py:65
  8.8 28.9 %all-to-all-start = ((bf16[8,8,128]{2,0,1:T(8,128)(2,1)}), bf16[8,8,128]{2,0,1:T(8,128)(2,1)S(1)}, u32[]{:S(2)}, u32[]{:S(2)}) async-start(bf16[8,8,128]{2,0,1:T(8,128)(2,1)} %bitcast.208), calls=%async_computation | async-start | bytes 32768 | tf_op jit(solution)/shard_map/all_to_all | solution.py:66
  15.6 131.7 %reduce-scatter.9.cloned.1.call-start = ((), (), s32[]{:S(2)}) async-start(), calls=%async_computation.15 | async-start | bytes 4718592 | tf_op jit(solution)/shard_map/reduce_scatter | solution.py:105
  15.6 39.3 %collective-permute-start = (bf16[16,1024]{1,0:T(8,128)(2,1)}, bf16[16,1024]{1,0:T(8,128)(2,1)S(1)}, u32[]{:S(2)}, u32[]{:S(2)}) collective-permute-start(bf16[16,1024]{1,0:T(8,128)(2,1)} %param.19), channel_id=1, source_target_pairs={{0,0},{8,1},{16,2},{24,3},{32,4},{40,5},{48,6},{56,7},{1,8},{9,9},... | collective-permute-start | bytes 98312 | tf_op jit(solution)/shard_map/ppermute | solution.py:67
  114.7 61.4 %all-gather.13.cloned.1.call-start = ((), (), s32[]{:S(2)}) async-start(), calls=%async_computation.17 | async-start | bytes 2228224 | tf_op jit(solution)/shard_map/all_gather | solution.py:65
  124.4 69.0 %all-gather.11.cloned.1.call-start = ((), (), s32[]{:S(2)}) async-start(), calls=%async_computation.16 | async-start | bytes 2359296 | tf_op jit(solution)/shard_map/all_gather | solution.py:65
  150.0 86.2 %all-gather.15.cloned.1.call-start = ((), (), s32[]{:S(2)}) async-start(), calls=%async_computation.18 | async-start | bytes 1114112 | tf_op jit(solution)/shard_map/all_gather | solution.py:65
  161.9 102.9 %all-gather.21.cloned.1.call-start = ((), (), s32[]{:S(2)}) async-start(), calls=%async_computation.28 | async-start | bytes 2359296 | tf_op jit(solution)/shard_map/all_gather | solution.py:65
  270.7 8.0 %all-to-all-start.3 = ((f32[8,128,1]{1,2,0:T(1,128)}), f32[8,128,1]{1,2,0:T(1,128)S(1)}, u32[]{:S(2)}, u32[]{:S(2)}) async-start(f32[8,128,1]{1,2,0:T(1,128)} %bitcast.30), calls=%async_computation.6 | async-start | bytes 8192 | tf_op jit(solution)/shard_map/all_to_all | solution.py:66
  274.1 63.5 %reduce-scatter.13.cloned.1.call-start = ((), (), s32[]{:S(2)}) async-start(), calls=%async_computation.20 | async-start | bytes 4718592 | tf_op jit(solution)/shard_map/reduce_scatter | solution.py:105
  303.2 66.2 %all-gather.17.cloned.1.call-start = ((), (), s32[]{:S(2)}) async-start(), calls=%async_computation.21 | async-start | bytes 2359296 | tf_op jit(solution)/shard_map/all_gather | solution.py:65
  341.6 103.3 %reduce-scatter.23.cloned.1.call-start = ((), (), s32[]{:S(2)}) async-start(), calls=%async_computation.26 | async-start | bytes 2228224 | tf_op jit(solution)/shard_map/reduce_scatter | solution.py:165
  346.3 179.1 %reduce-scatter.21.cloned.1.call-start = ((), (), s32[]{:S(2)}) async-start(), calls=%async_computation.25 | async-start | bytes 4456448 | tf_op jit(solution)/shard_map/reduce_scatter | solution.py:165
  352.8 247.7 %reduce-scatter.17.cloned.1.call-start = ((), (), s32[]{:S(2)}) async-start(), calls=%async_computation.23 | async-start | bytes 1114112 | tf_op jit(solution)/shard_map/reduce_scatter | solution.py:165
  406.0 269.4 %reduce-scatter.19.cloned.1.call-start = ((), (), s32[]{:S(2)}) async-start(), calls=%async_computation.24 | async-start | bytes 557056 | tf_op jit(solution)/shard_map/reduce_scatter | solution.py:165
  408.9 305.2 %reduce-scatter.15.cloned.1.call-start = ((), (), s32[]{:S(2)}) async-start(), calls=%async_computation.22 | async-start | bytes 4718592 | tf_op jit(solution)/shard_map/reduce_scatter | solution.py:105
  412.9 371.4 %reduce-scatter.11.cloned.1.call-start = ((), (), s32[]{:S(2)}) async-start(), calls=%async_computation.19 | async-start | bytes 4718592 | tf_op jit(solution)/shard_map/reduce_scatter | solution.py:105
  417.5 264.9 %copy-start.4 = (bf16[128,1024]{1,0:T(8,128)(2,1)S(1)}, bf16[128,1024]{1,0:T(8,128)(2,1)}, u32[]{:S(2)}) copy-start(bf16[128,1024]{1,0:T(8,128)(2,1)} %multiply_convert_fusion.4) | copy-start | bytes 786436
  417.5 264.9 %copy-start.35 = (bf16[128,8]{0,1:T(8,128)(2,1)S(1)}, bf16[128,8]{0,1:T(8,128)(2,1)}, u32[]{:S(2)}) copy-start(bf16[128,8]{0,1:T(8,128)(2,1)} %multiply_convert_fusion.6) | copy-start | bytes 6148
  417.5 266.7 %copy-start.54 = (f32[128]{0:T(128)S(1)}, f32[128]{0:T(128)}, u32[]{:S(2)}) copy-start(f32[128]{0:T(128)} %get-tuple-element.11) | copy-start | bytes 1540
  417.5 266.8 %copy-start.56 = (f32[64]{0:T(128)S(1)}, f32[64]{0:T(128)}, u32[]{:S(2)}) copy-start(f32[64]{0:T(128)} %get-tuple-element.13) | copy-start | bytes 772
  417.5 296.6 %copy-start.33 = (f32[1024]{0:T(1024)S(1)}, f32[1024]{0:T(1024)}, u32[]{:S(2)}) copy-start(f32[1024]{0:T(1024)} %copy-done.31) | copy-start | bytes 12292
  417.5 297.9 %copy-start.36 = (f32[1024]{0:T(1024)S(1)}, f32[1024]{0:T(1024)}, u32[]{:S(2)}) copy-start(f32[1024]{0:T(1024)} %get-tuple-element.15) | copy-start | bytes 12292
  417.6 366.7 %copy-start.7 = (bf16[1,128,1024]{2,1,0:T(8,128)(2,1)S(1)}, bf16[1,128,1024]{2,1,0:T(8,128)(2,1)}, u32[]{:S(2)}) copy-start(bf16[1,128,1024]{2,1,0:T(8,128)(2,1)} %param.28) | copy-start | bytes 786436
  417.6 366.7 %copy-start.25 = (f32[1024]{0:T(1024)S(1)}, f32[1024]{0:T(1024)}, u32[]{:S(2)}) copy-start(f32[1024]{0:T(1024)} %copy-done.24) | copy-start | bytes 12292
  417.6 366.7 %copy-start.42 = (f32[128]{0:T(128)S(1)}, f32[128]{0:T(128)}, u32[]{:S(2)}) copy-start(f32[128]{0:T(128)} %copy-done.41) | copy-start | bytes 1540
  417.6 366.7 %copy-start.50 = (f32[128]{0:T(128)S(1)}, f32[128]{0:T(128)}, u32[]{:S(2)}) copy-start(f32[128]{0:T(128)} %copy-done.49) | copy-start | bytes 1540
  417.6 370.2 %copy-start.1 = (bf16[1024,8]{0,1:T(8,128)(2,1)S(1)}, bf16[1024,8]{0,1:T(8,128)(2,1)}, u32[]{:S(2)}) copy-start(bf16[1024,8]{0,1:T(8,128)(2,1)} %param.23) | copy-start | bytes 49156
  446.6 80.7 %all-to-all-start.6 = ((f32[64,1,512]{2,1,0:T(1,128)}), f32[64,1,512]{2,1,0:T(1,128)S(1)}, u32[]{:S(2)}, u32[]{:S(2)}) async-start(f32[64,1,512]{2,1,0:T(1,128)} %copy.68), calls=%async_computation.14 | async-start | bytes 262144 | tf_op jit(solution)/shard_map/all_to_all | solution.py:66
  527.3 78.3 %all-to-all-start.5 = ((f32[64,1,1024]{2,1,0:T(1,128)}), f32[64,1,1024]{2,1,0:T(1,128)S(1)}, u32[]{:S(2)}, u32[]{:S(2)}) async-start(f32[64,1,1024]{2,1,0:T(1,128)} %copy.66), calls=%async_computation.12 | async-start | bytes 524288 | tf_op jit(solution)/shard_map/all_to_all | solution.py:66
  600.6 86.6 %collective-permute-start.1 = (f32[16,1024]{1,0:T(8,128)}, f32[16,1024]{1,0:T(8,128)S(1)}, u32[]{:S(2)}, u32[]{:S(2)}) collective-permute-start(f32[16,1024]{1,0:T(8,128)} %reduce-scatter.17.cloned.1.call-done), channel_id=1, source_target_pairs={{0,0},{1,8},{2,16},{3,24},{4,32},{5,40},{6,48},{7,56},{8,1},{9,9},... | collective-permute-start | bytes 196616 | tf_op jit(solution)/shard_map/ppermute | solution.py:166
  675.4 11.7 %all-to-all-start.4 = ((f32[8,8,128]{2,1,0:T(8,128)}), f32[8,8,128]{2,1,0:T(8,128)S(1)}, u32[]{:S(2)}, u32[]{:S(2)}) async-start(f32[8,8,128]{2,1,0:T(8,128)} %bitcast.198), calls=%async_computation.10 | async-start | bytes 65536 | tf_op jit(solution)/shard_map/all_to_all | solution.py:66
  (51 other events, 885.8 us)
Sparse Core Ops, SparseCore 0:
  10.6 28.9 all-gather.18
  114.8 32.4 reduce-scatter.8
  303.3 34.2 reduce-scatter.12
Sparse Core Ops, SparseCore 1:
  124.5 39.9 all-gather.12
  166.6 26.8 all-gather.10
  195.5 40.6 all-gather.14
  237.9 26.9 all-gather.20
  341.6 27.7 all-gather.16
  372.6 72.2 reduce-scatter.22
  448.5 76.8 reduce-scatter.20
  528.4 72.1 reduce-scatter.16
  603.9 71.4 reduce-scatter.18
  677.8 36.2 reduce-scatter.14
  716.4 37.5 reduce-scatter.10
where the time goes:
time: 803 us; the launch traced here: 795 us
  waiting for transfers between devices  424 us (53%)
  blocking collectives  199 us (25%)
  matrix products  73.4 us (9%)
  starting transfers between devices  39.8 us (5%)
  other arithmetic  32.9 us (4%)
  between operations  16.8 us (2%)
  local copies, waits for them, and re-layouts  10.3 us (1%)
    reduce_scatter x4, waiting for transfers between devices, local(): rss = lambda t: lax.psum_scatter(t, 'seq', scatter_dimension=0, tiled=True)  236 us
    all_gather x6, waiting for transfers between devices, local(): ag = lambda v, ax: lax.all_gather(v, ax, axis=0, tiled=True)  95.8 us
    reduce_scatter x4, waiting for transfers between devices, local(): rs = lambda t: lax.psum_scatter(t, 'ctx', scatter_dimension=0, tiled=True)  83.6 us
    all_gather x5, blocking collectives, local(): ag = lambda v, ax: lax.all_gather(v, ax, axis=0, tiled=True)  73.5 us
    psum x1, blocking collectives, local(): lax.psum((attn_loc, gq_all, gk_all, mlp_loc, router_loc), ('seq', 'ctx'))  68.8 us
    dot_general x14, matrix products, dot(): lax.dot_general(a, b, (((ca,), (cb,)), ((), ())), preferred_element_type=...  50.5 us
    all_to_all x5, starting transfers between devices, local(): a2a = lambda v, sp, cc: lax.all_to_all(v, 'ctx', sp, cc, tiled=True)  30.9 us
    psum x1, blocking collectives, local(): sums = lax.psum(jnp.stack([jnp.sum(q * q, 1), jnp.sum(k * k, 1)]), 'ctx')  22.6 us
  transfers between devices with their start and end apart: 21, of which 13 were waited for; matrix products, arithmetic and copies ran while one was open for 9% of the time, Pallas kernels for 0%

commit v1 on v0

--- a/solution.py
+++ b/solution.py
@@ -78,7 +78,9 @@
     x_low = (x * s1 * attn_gain_f).astype(BF16)
     qkv = dot(x_low, w_qkv, 1, 1)
     q, k, v = (qkv[:, :128], qkv[:, 128:192], qkv[:, 192:])
-    sums = lax.psum(jnp.stack([jnp.sum(q * q, 1), jnp.sum(k * k, 1)]), "ctx")
+    value = jnp.stack([jnp.sum(q * q, 1), jnp.sum(k * k, 1)])
+    parts = lax.all_gather(value, "ctx", axis=0, tiled=False)
+    sums = parts.sum(axis=0)
     sq = lax.rsqrt(sums[0] / 1024 + EPSILON)[:, None]
     sk = lax.rsqrt(sums[1] / 512 + EPSILON)[:, None]
     nq, nk = (q * sq, k * sk)

time: 803 us -> 802 us (level)
    all_gather x0 -> x1, blocking collectives: none -> 23.2 us  [local(): parts = lax.all_gather(value, 'ctx', axis=0, tiled=False)]
    psum x1 -> x0, blocking collectives: 22.6 us -> none  [local(): sums = lax.psum(jnp.stack([jnp.sum(q * q, 1), jnp.sum(k * k, 1)]), 'ctx')]
where the time goes in v1:
time: 802 us; the launch traced here: 794 us
  waiting for transfers between devices  424 us (53%)
  blocking collectives  198 us (25%)
  matrix products  73.5 us (9%)
  starting transfers between devices  39.9 us (5%)
  other arithmetic  31.1 us (4%)
  between operations  16.8 us (2%)
  local copies, waits for them, and re-layouts  10.7 us (1%)
    reduce_scatter x4, waiting for transfers between devices, local(): rss = lambda t: lax.psum_scatter(t, 'seq', scatter_dimension=0, tiled=True)  236 us
    all_gather x6, waiting for transfers between devices, local(): ag = lambda v, ax: lax.all_gather(v, ax, axis=0, tiled=True)  95.8 us
    reduce_scatter x4, waiting for transfers between devices, local(): rs = lambda t: lax.psum_scatter(t, 'ctx', scatter_dimension=0, tiled=True)  84.2 us
    all_gather x5, blocking collectives, local(): ag = lambda v, ax: lax.all_gather(v, ax, axis=0, tiled=True)  73.5 us
    psum x1, blocking collectives, local(): lax.psum((attn_loc, gq_all, gk_all, mlp_loc, router_loc), ('seq', 'ctx'))  68.7 us
    dot_general x14, matrix products, dot(): lax.dot_general(a, b, (((ca,), (cb,)), ((), ())), preferred_element_type=...  50.6 us
    all_to_all x5, starting transfers between devices, local(): a2a = lambda v, sp, cc: lax.all_to_all(v, 'ctx', sp, cc, tiled=True)  30.9 us
    all_gather x1, blocking collectives, local(): parts = lax.all_gather(value, 'ctx', axis=0, tiled=False)  23.2 us
  transfers between devices with their start and end apart: 21, of which 13 were waited for; matrix products, arithmetic and copies ran while one was open for 9% of the time, Pallas kernels for 0%

profile of v1, /device:TPU:1, one launch (start us, length us, event | category | flops | bytes accessed | tf_op | source)
XLA Modules:
  0.0 794.2 jit_solution(3438188153228695705)
XLA Ops:
  8.8 6.8 all-to-all-start
  23.2 13.3 %all-gather.2 = s32[1,1024]{1,0:T(1,128)S(1)} all-gather(s32[1,128]{1,0:T(1,128)} %param.16), channel_id=4, replica_groups=mesh['seq'=16,'ctx'=8] {'ctx'}, dimensions={1}, use_global_device_ids=true | all-gather | bytes 4608 | tf_op jit(solution)/shard_map/all_gather | solution.py:65
  36.5 17.2 %all_gather.44 = bf16[1024,128]{1,0:T(8,128)(2,1)S(1)} all-gather(bf16[64,128]{1,0:T(8,128)(2,1)S(1)} %bitcast.195), channel_id=1, replica_groups=mesh['seq'=16,'ctx'=8] {'seq'}, dimensions={0}, use_global_device_ids=true | all-gather | bytes 278528 | tf_op jit(solution)/shard_map/all_gather | solution.py:65
  53.8 17.4 %all_gather.40 = bf16[256,1024]{1,0:T(8,128)(2,1)S(1)} all-gather(bf16[16,1024]{1,0:T(8,128)(2,1)S(1)} %collective-permute-done), channel_id=1, replica_groups=mesh['seq'=16,'ctx'=8] {'seq'}, dimensions={0}, use_global_device_ids=true | all-gather | bytes 557056 | tf_op jit(solution)/shard_map/all_gather | solution.py:65
  76.1 23.2 %all-gather.5 = f32[8,2,1024]{2,1,0:T(2,128)S(1)} all-gather(f32[1,2,1024]{2,1,0:T(2,128)S(1)} %maximum_bitcast_fusion.6), channel_id=3, replica_groups=mesh['seq'=16,'ctx'=8] {'ctx'}, dimensions={0}, use_global_device_ids=true | all-gather | bytes 73728 | tf_op jit(solution)/shard_map/all_gather | solution.py:82
  101.2 5.5 fusion.97
  114.0 8.5 %all_to_all.120 = bf16[8,8,1024]{2,0,1:T(8,128)(2,1)} all-to-all(bf16[8,8,1024]{2,0,1:T(8,128)(2,1)S(1)} %copy.58), channel_id=1, replica_groups=mesh['seq'=16,'ctx'=8] {'ctx'}, dimensions={1} | all-to-all | bytes 262144 | tf_op jit(solution)/shard_map/all_to_all | solution.py:66
  122.6 23.4 %reduce-scatter.9.cloned.1.call-done = f32[128,1024]{1,0:T(8,128)} async-done(((f32[1024,1024]{1,0:T(8,128)}), f32[128,1024]{1,0:T(8,128)}) %reduce-scatter.9.cloned.1.call-update) | async-done | bytes 524304 | tf_op jit(solution)/shard_map/reduce_scatter | solution.py:107
  148.8 11.8 %all_to_all.121 = bf16[8,8,512]{2,0,1:T(8,128)(2,1)} all-to-all(bf16[8,8,512]{2,0,1:T(8,128)(2,1)S(1)} %copy.59), channel_id=1, replica_groups=mesh['seq'=16,'ctx'=8] {'ctx'}, dimensions={1} | all-to-all | bytes 131072 | tf_op jit(solution)/shard_map/all_to_all | solution.py:66
  161.3 12.3 %all-gather.3 = s32[1,1024,4]{1,2,0:T(4,128)S(1)} all-gather(s32[1,128,4]{1,2,0:T(4,128)S(1)} %copy-done.53), channel_id=5, replica_groups=mesh['seq'=16,'ctx'=8] {'ctx'}, dimensions={1}, use_global_device_ids=true | all-gather | bytes 18432 | tf_op jit(solution)/shard_map/all_gather | solution.py:65
  174.8 17.4 %all-gather.13.cloned.1.call-done = bf16[1024,1024]{1,0:T(8,128)(2,1)} async-done(((bf16[128,1024]{1,0:T(8,128)(2,1)}), bf16[1024,1024]{1,0:T(8,128)(2,1)}) %all-gather.13.cloned.1.call-update) | async-done | bytes 2097168 | tf_op jit(solution)/shard_map/all_gather | solution.py:65
  192.1 6.5 fusion.100
  201.5 33.3 %all-gather.17.cloned.1.call-done = bf16[1024,512]{1,0:T(8,128)(2,1)} async-done(((bf16[64,512]{1,0:T(8,128)(2,1)}), bf16[1024,512]{1,0:T(8,128)(2,1)}) %all-gather.17.cloned.1.call-update) | async-done | bytes 1048592 | tf_op jit(solution)/shard_map/all_gather | solution.py:65
  234.9 28.7 %all-gather.23.cloned.1.call-done = bf16[1,1024,1024]{2,1,0:T(8,128)(2,1)} async-done(((bf16[1,128,1024]{2,1,0:T(8,128)(2,1)}), bf16[1,1024,1024]{2,1,0:T(8,128)(2,1)}) %all-gather.23.cloned.1.call-update) | async-done | bytes 2097168 | tf_op jit(solution)/shard_map/all_gather | solution.py:65
  263.5 5.2 fusion.9
  277.4 13.3 %all_gather.46 = f32[1024,8]{0,1:T(8,128)S(1)} all-gather(f32[128,8]{0,1:T(8,128)S(1)} %get-tuple-element.25), channel_id=1, replica_groups=mesh['seq'=16,'ctx'=8] {'ctx'}, dimensions={0}, use_global_device_ids=true | all-gather | bytes 36864 | tf_op jit(solution)/shard_map/all_gather | solution.py:65
  290.7 5.4 multiply_convert_fusion.1
  302.5 33.9 %reduce-scatter.13.cloned.1.call-done = f32[128,1024]{1,0:T(8,128)} async-done(((f32[1024,1024]{1,0:T(8,128)}), f32[128,1024]{1,0:T(8,128)}) %reduce-scatter.13.cloned.1.call-update) | async-done | bytes 524304 | tf_op jit(solution)/shard_map/reduce_scatter | solution.py:107
  345.1 6.5 fusion.19
  351.7 16.4 %all-gather.19.cloned.1.call-done = bf16[1024,1024]{1,0:T(8,128)(2,1)} async-done(((bf16[128,1024]{1,0:T(8,128)(2,1)}), bf16[1024,1024]{1,0:T(8,128)(2,1)}) %all-gather.19.cloned.1.call-update) | async-done | bytes 2097168 | tf_op jit(solution)/shard_map/all_gather | solution.py:65
  383.4 12.2 %psum.42 = f32[2,1024]{1,0:T(2,128)S(1)} all-reduce(f32[2,1024]{1,0:T(2,128)S(1)} %pad_maximum_fusion.16), channel_id=1, replica_groups=mesh['seq'=16,'ctx'=8] {'ctx'}, use_global_device_ids=true, to_apply=%region_21.22 | all-reduce | flops 2048 | bytes 16384 | tf_op jit(solution)/shard_map/psum | solution.py:157
  397.2 5.0 fusion.29
  416.4 27.3 %reduce-scatter.23.cloned.1.call-done = f32[64,512]{1,0:T(8,128)} async-done(((f32[1024,512]{1,0:T(8,128)}), f32[64,512]{1,0:T(8,128)}) %reduce-scatter.23.cloned.1.call-update) | async-done | bytes 131088 | tf_op jit(solution)/shard_map/reduce_scatter | solution.py:167
  445.4 6.7 all-to-all-start.6
  452.2 72.1 %reduce-scatter.21.cloned.1.call-done = f32[64,1024]{1,0:T(8,128)} async-done(((f32[1024,1024]{1,0:T(8,128)}), f32[64,1024]{1,0:T(8,128)}) %reduce-scatter.21.cloned.1.call-update) | async-done | bytes 262160 | tf_op jit(solution)/shard_map/reduce_scatter | solution.py:167
  526.2 6.8 all-to-all-start.5
  533.0 66.5 %reduce-scatter.17.cloned.1.call-done = f32[16,1024]{1,0:T(8,128)} async-done(((f32[256,1024]{1,0:T(8,128)}), f32[16,1024]{1,0:T(8,128)}) %reduce-scatter.17.cloned.1.call-update) | async-done | bytes 65552 | tf_op jit(solution)/shard_map/reduce_scatter | solution.py:167
  599.5 5.0 collective-permute-start.1
  604.5 69.7 %reduce-scatter.19.cloned.1.call-done = f32[64,128]{1,0:T(8,128)} async-done(((f32[1024,128]{1,0:T(8,128)}), f32[64,128]{1,0:T(8,128)}) %reduce-scatter.19.cloned.1.call-update) | async-done | bytes 32784 | tf_op jit(solution)/shard_map/reduce_scatter | solution.py:167
  674.3 7.0 all-to-all-start.4
  686.0 26.9 %reduce-scatter.15.cloned.1.call-done = f32[128,1024]{1,0:T(8,128)} async-done(((f32[1024,1024]{1,0:T(8,128)}), f32[128,1024]{1,0:T(8,128)}) %reduce-scatter.15.cloned.1.call-update) | async-done | bytes 524304 | tf_op jit(solution)/shard_map/reduce_scatter | solution.py:107
  714.3 68.7 %all-reduce = (f32[1024,8]{0,1:T(8,128)}, f32[1024]{0:T(1024)}, f32[1024]{0:T(1024)}, f32[512]{0:T(512)}, f32[1024]{0:T(1024)}) all-reduce(f32[1024,8]{0,1:T(8,128)S(1)} %fusion.102, f32[1024]{0:T(1024)S(1)} %get-tuple-element.17, f32[1024]{0:T(1024)S(1)} %dynamic_update_slice.6, ...), channel_id=1, replica_groups=mesh['seq'=16,'ctx'=8] {'seq','ctx'}, use_global_device_ids=true, to_apply=%region_28.29 | all-reduce | flops 11776 | bytes 94208 | tf_op jit(solution)/shard_map/psum | solution.py:174
  (244 shorter events, 97.2 us)
Async XLA Ops:
  8.0 63.2 %all-gather.21.cloned.1.call-start = ((), (), s32[]{:S(2)}) async-start(), calls=%async_computation.27 | async-start | bytes 2359296 | tf_op jit(solution)/shard_map/all_gather | solution.py:65
  8.8 27.8 %all-to-all-start = ((bf16[8,8,128]{2,0,1:T(8,128)(2,1)}), bf16[8,8,128]{2,0,1:T(8,128)(2,1)S(1)}, u32[]{:S(2)}, u32[]{:S(2)}) async-start(bf16[8,8,128]{2,0,1:T(8,128)(2,1)} %bitcast.210), calls=%async_computation | async-start | bytes 32768 | tf_op jit(solution)/shard_map/all_to_all | solution.py:66
  15.6 130.4 %reduce-scatter.9.cloned.1.call-start = ((), (), s32[]{:S(2)}) async-start(), calls=%async_computation.15 | async-start | bytes 4718592 | tf_op jit(solution)/shard_map/reduce_scatter | solution.py:107
  15.6 38.2 %collective-permute-start = (bf16[16,1024]{1,0:T(8,128)(2,1)}, bf16[16,1024]{1,0:T(8,128)(2,1)S(1)}, u32[]{:S(2)}, u32[]{:S(2)}) collective-permute-start(bf16[16,1024]{1,0:T(8,128)(2,1)} %param.19), channel_id=1, source_target_pairs={{0,0},{8,1},{16,2},{24,3},{32,4},{40,5},{48,6},{56,7},{1,8},{9,9},... | collective-permute-start | bytes 98312 | tf_op jit(solution)/shard_map/ppermute | solution.py:67
  113.9 60.9 %all-gather.15.cloned.1.call-start = ((), (), s32[]{:S(2)}) async-start(), calls=%async_computation.17 | async-start | bytes 2228224 | tf_op jit(solution)/shard_map/all_gather | solution.py:65
  122.5 69.6 %all-gather.13.cloned.1.call-start = ((), (), s32[]{:S(2)}) async-start(), calls=%async_computation.16 | async-start | bytes 2359296 | tf_op jit(solution)/shard_map/all_gather | solution.py:65
  148.7 86.2 %all-gather.17.cloned.1.call-start = ((), (), s32[]{:S(2)}) async-start(), calls=%async_computation.18 | async-start | bytes 1114112 | tf_op jit(solution)/shard_map/all_gather | solution.py:65
  160.6 102.9 %all-gather.23.cloned.1.call-start = ((), (), s32[]{:S(2)}) async-start(), calls=%async_computation.28 | async-start | bytes 2359296 | tf_op jit(solution)/shard_map/all_gather | solution.py:65
  269.4 8.0 %all-to-all-start.3 = ((f32[8,128,1]{1,2,0:T(1,128)}), f32[8,128,1]{1,2,0:T(1,128)S(1)}, u32[]{:S(2)}, u32[]{:S(2)}) async-start(f32[8,128,1]{1,2,0:T(1,128)} %bitcast.31), calls=%async_computation.6 | async-start | bytes 8192 | tf_op jit(solution)/shard_map/all_to_all | solution.py:66
  272.8 63.5 %reduce-scatter.13.cloned.1.call-start = ((), (), s32[]{:S(2)}) async-start(), calls=%async_computation.20 | async-start | bytes 4718592 | tf_op jit(solution)/shard_map/reduce_scatter | solution.py:107
  301.9 66.2 %all-gather.19.cloned.1.call-start = ((), (), s32[]{:S(2)}) async-start(), calls=%async_computation.21 | async-start | bytes 2359296 | tf_op jit(solution)/shard_map/all_gather | solution.py:65
  340.3 103.4 %reduce-scatter.23.cloned.1.call-start = ((), (), s32[]{:S(2)}) async-start(), calls=%async_computation.26 | async-start | bytes 2228224 | tf_op jit(solution)/shard_map/reduce_scatter | solution.py:167
  345.1 179.2 %reduce-scatter.21.cloned.1.call-start = ((), (), s32[]{:S(2)}) async-start(), calls=%async_computation.25 | async-start | bytes 4456448 | tf_op jit(solution)/shard_map/reduce_scatter | solution.py:167
  351.6 247.8 %reduce-scatter.17.cloned.1.call-start = ((), (), s32[]{:S(2)}) async-start(), calls=%async_computation.23 | async-start | bytes 1114112 | tf_op jit(solution)/shard_map/reduce_scatter | solution.py:167
  404.8 269.4 %reduce-scatter.19.cloned.1.call-start = ((), (), s32[]{:S(2)}) async-start(), calls=%async_computation.24 | async-start | bytes 557056 | tf_op jit(solution)/shard_map/reduce_scatter | solution.py:167
  407.7 305.3 %reduce-scatter.15.cloned.1.call-start = ((), (), s32[]{:S(2)}) async-start(), calls=%async_computation.22 | async-start | bytes 4718592 | tf_op jit(solution)/shard_map/reduce_scatter | solution.py:107
  411.7 371.3 %reduce-scatter.11.cloned.1.call-start = ((), (), s32[]{:S(2)}) async-start(), calls=%async_computation.19 | async-start | bytes 4718592 | tf_op jit(solution)/shard_map/reduce_scatter | solution.py:107
  416.3 265.0 %copy-start.4 = (bf16[128,1024]{1,0:T(8,128)(2,1)S(1)}, bf16[128,1024]{1,0:T(8,128)(2,1)}, u32[]{:S(2)}) copy-start(bf16[128,1024]{1,0:T(8,128)(2,1)} %multiply_convert_fusion.4) | copy-start | bytes 786436
  416.3 265.0 %copy-start.36 = (bf16[128,8]{0,1:T(8,128)(2,1)S(1)}, bf16[128,8]{0,1:T(8,128)(2,1)}, u32[]{:S(2)}) copy-start(bf16[128,8]{0,1:T(8,128)(2,1)} %multiply_convert_fusion.6) | copy-start | bytes 6148
  416.3 266.7 %copy-start.56 = (f32[128]{0:T(128)S(1)}, f32[128]{0:T(128)}, u32[]{:S(2)}) copy-start(f32[128]{0:T(128)} %get-tuple-element.11) | copy-start | bytes 1540
  416.3 266.9 %copy-start.58 = (f32[64]{0:T(128)S(1)}, f32[64]{0:T(128)}, u32[]{:S(2)}) copy-start(f32[64]{0:T(128)} %get-tuple-element.13) | copy-start | bytes 772
  416.3 296.6 %copy-start.33 = (f32[1024]{0:T(1024)S(1)}, f32[1024]{0:T(1024)}, u32[]{:S(2)}) copy-start(f32[1024]{0:T(1024)} %copy-done.31) | copy-start | bytes 12292
  416.4 297.9 %copy-start.37 = (f32[1024]{0:T(1024)S(1)}, f32[1024]{0:T(1024)}, u32[]{:S(2)}) copy-start(f32[1024]{0:T(1024)} %get-tuple-element.15) | copy-start | bytes 12292
  416.4 366.6 %copy-start.7 = (bf16[1,128,1024]{2,1,0:T(8,128)(2,1)S(1)}, bf16[1,128,1024]{2,1,0:T(8,128)(2,1)}, u32[]{:S(2)}) copy-start(bf16[1,128,1024]{2,1,0:T(8,128)(2,1)} %param.28) | copy-start | bytes 786436
  416.4 366.6 %copy-start.25 = (f32[1024]{0:T(1024)S(1)}, f32[1024]{0:T(1024)}, u32[]{:S(2)}) copy-start(f32[1024]{0:T(1024)} %copy-done.24) | copy-start | bytes 12292
  416.4 366.6 %copy-start.43 = (f32[128]{0:T(128)S(1)}, f32[128]{0:T(128)}, u32[]{:S(2)}) copy-start(f32[128]{0:T(128)} %copy-done.42) | copy-start | bytes 1540
  416.4 366.6 %copy-start.51 = (f32[128]{0:T(128)S(1)}, f32[128]{0:T(128)}, u32[]{:S(2)}) copy-start(f32[128]{0:T(128)} %copy-done.50) | copy-start | bytes 1540
  416.4 370.2 %copy-start.1 = (bf16[1024,8]{0,1:T(8,128)(2,1)S(1)}, bf16[1024,8]{0,1:T(8,128)(2,1)}, u32[]{:S(2)}) copy-start(bf16[1024,8]{0,1:T(8,128)(2,1)} %param.23) | copy-start | bytes 49156
  445.4 80.7 %all-to-all-start.6 = ((f32[64,1,512]{2,1,0:T(1,128)}), f32[64,1,512]{2,1,0:T(1,128)S(1)}, u32[]{:S(2)}, u32[]{:S(2)}) async-start(f32[64,1,512]{2,1,0:T(1,128)} %copy.68), calls=%async_computation.14 | async-start | bytes 262144 | tf_op jit(solution)/shard_map/all_to_all | solution.py:66
  526.2 78.4 %all-to-all-start.5 = ((f32[64,1,1024]{2,1,0:T(1,128)}), f32[64,1,1024]{2,1,0:T(1,128)S(1)}, u32[]{:S(2)}, u32[]{:S(2)}) async-start(f32[64,1,1024]{2,1,0:T(1,128)} %copy.66), calls=%async_computation.12 | async-start | bytes 524288 | tf_op jit(solution)/shard_map/all_to_all | solution.py:66
  599.5 86.5 %collective-permute-start.1 = (f32[16,1024]{1,0:T(8,128)}, f32[16,1024]{1,0:T(8,128)S(1)}, u32[]{:S(2)}, u32[]{:S(2)}) collective-permute-start(f32[16,1024]{1,0:T(8,128)} %reduce-scatter.17.cloned.1.call-done), channel_id=1, source_target_pairs={{0,0},{1,8},{2,16},{3,24},{4,32},{5,40},{6,48},{7,56},{8,1},{9,9},... | collective-permute-start | bytes 196616 | tf_op jit(solution)/shard_map/ppermute | solution.py:168
  674.3 11.7 %all-to-all-start.4 = ((f32[8,8,128]{2,1,0:T(8,128)}), f32[8,8,128]{2,1,0:T(8,128)S(1)}, u32[]{:S(2)}, u32[]{:S(2)}) async-start(f32[8,8,128]{2,1,0:T(8,128)} %bitcast.200), calls=%async_computation.10 | async-start | bytes 65536 | tf_op jit(solution)/shard_map/all_to_all | solution.py:66
  (53 other events, 1056.5 us)
Sparse Core Ops, SparseCore 0:
  10.6 28.9 all-gather.20
  114.0 31.9 reduce-scatter.8
  302.0 34.3 reduce-scatter.12
Sparse Core Ops, SparseCore 1:
  122.6 40.5 all-gather.14
  165.3 26.8 all-gather.12
  194.2 40.6 all-gather.16
  236.6 26.9 all-gather.22
  340.4 27.7 all-gather.18
  371.4 72.2 reduce-scatter.22
  447.3 76.9 reduce-scatter.20
  527.3 72.1 reduce-scatter.16
  602.9 71.3 reduce-scatter.18
  676.7 36.2 reduce-scatter.14
  715.2 37.0 reduce-scatter.10
